TPU v7x, 512 devices: a whole 4x8x8 slice. The times are simulated.
512 devices in a mesh: section: 4 (over x), rep: 128 (over y, z, core).
Axes of the slice: x: 4, y: 8, z: 8, core: 2. Of those that a mesh axis runs over, the one named last changes fastest.
Arguments:
- tile_features: bfloat16 [256, 16, 16, 512], P('rep'), may hold values from -6 to 6
- patches: bfloat16 [256, 16, 16, 768], P('rep'), may hold values from -6 to 6
- det_kernel: float32 [4, 7, 7, 512], P('section'), may hold values from -0.875 to 0.875
- det_gain: float32 [4, 512], P('section'), may hold values from 0.1 to 1.9
- det_in: bfloat16 [4, 512, 2048], P('section', None, 'rep'), may hold values from -0.25 to 0.25
- det_out: bfloat16 [4, 2048, 512], P('section', 'rep'), may hold values from -0.125 to 0.125
- det_scale: float32 [4, 512], P('section'), may hold values from 0.3 to 1.5
- cls_embed: bfloat16 [768, 1024], P(None, 'section'), may hold values from -0.21875 to 0.21875
- cls_merge: bfloat16 [512, 1024], P(None, 'section'), may hold values from -0.25 to 0.25
- cls_pos: bfloat16 [196, 1024], P(None, 'section'), may hold values from -3 to 3
- cls_qkv: bfloat16 [1024, 3, 512], P(None, None, 'section'), may hold values from -1.5 to 1.5
- cls_out: bfloat16 [512, 1024], P('section'), may hold values from -0.25 to 0.25
- cls_gain: float32 [2, 1024], replicated, may hold values from 0.1 to 1.9
- crop_plan: int32 [128, 4, 3, 3], P('rep'), may hold values from 0 to 2, as said below
- slot_from: int32 [128, 4], P('rep'), may hold values from 0 to 3, as said below
Outputs:
- crop_class: float32 [128, 4, 1024], P('rep', 'section')
Inputs may be any that keep to these rules, and one draw needn't show every extreme that they name: `crop_plan`: each entry is a micro-batch below 2 followed by a top and a left patch offset of 0 to 2; records that no slot names are arbitrary. `slot_from`: 0 marks an empty slot, 1 a crop from the replica one index lower, 2 the replica's own, 3 one from the replica one index higher; the first replica never has 1 and the last never has 3.
All inputs are finite; a program needn't handle non-finite values.
Results may differ from a plain program's by a relative error of at most 0.004.
Values may be sent and summed in bfloat16 or wider, within the bound.
No kernel may reach another device: no remote copies, remote signals or barrier semaphores. Data moves between devices by JAX's collectives and lax.ppermute only.
A program may use at most 64 MiB of HBM per device.

v0:
```python
import math
import jax
import jax.numpy as jnp
from jax import lax
from jax.sharding import PartitionSpec as P

HEAD_DIM = 64
TILE = 16
CROP = 14
epsilon = 1e-06


def passed_along(block, axis, distance):
    devices = range(lax.axis_size(axis))
    route = [(i - distance, i) for i in devices if i - distance in devices]
    return lax.ppermute(block, axis, route)


def spread(value, axis, source):
    kept = jnp.where(lax.axis_index(axis) == source, value, 0).astype(value.dtype)
    return lax.psum(kept, axis)


def padded_2(block, sides, width):
    for axis, dim in sides:
        count = lax.axis_size(axis)
        forward = [(i, i + 1) for i in range(count - 1)]
        backward = [(target, source) for source, target in forward]
        low = lax.ppermute(
            lax.slice_in_dim(block, block.shape[dim] - width, None, axis=dim), axis, forward
        )
        high = lax.ppermute(lax.slice_in_dim(block, 0, width, axis=dim), axis, backward)
        block = jnp.concatenate([low, block, high], axis=dim)
    return block


def layer_norm(values, gain_row):
    row_mean = jnp.mean(values, axis=-1, keepdims=True)
    centred = values - row_mean
    row_var = jnp.mean(centred * centred, axis=-1, keepdims=True)
    return centred * lax.rsqrt(row_var + epsilon) * gain_row


def detector_block(tile_rows, kernel, gain_row, in_weight, out_weight, scale_row):
    widened = tile_rows.astype(jnp.float32)
    padded = jnp.pad(widened, ((3, 3), (3, 3), (0, 0)))
    conv = jnp.zeros_like(widened)
    for row_shift in range(7):
        for col_shift in range(7):
            conv = (
                conv
                + padded[row_shift : row_shift + TILE, col_shift : col_shift + TILE]
                * kernel[row_shift, col_shift]
            )
    normed = layer_norm(conv, gain_row).astype(jnp.bfloat16).reshape(TILE * TILE, -1)
    hidden = jax.nn.gelu(jnp.dot(normed, in_weight, preferred_element_type=jnp.float32)).astype(
        jnp.bfloat16
    )
    update = jnp.dot(hidden, out_weight, preferred_element_type=jnp.float32).reshape(widened.shape)
    return (widened + scale_row * update).astype(jnp.bfloat16)


def per_device(
    tile_features,
    patches,
    det_kernel,
    det_gain,
    det_in,
    det_out,
    det_scale,
    cls_embed,
    cls_merge,
    cls_pos,
    cls_qkv,
    cls_out,
    cls_gain,
    crop_plan,
    slot_from,
):
    sections = lax.axis_size("section")
    section_num = lax.axis_index("section")
    micro_count = tile_features.shape[0]
    in_whole, out_whole = (
        lax.all_gather(det_in, "rep", axis=2, tiled=True),
        lax.all_gather(det_out, "rep", axis=1, tiled=True),
    )
    kernel = det_kernel[0]
    gain_row = det_gain[0]
    scale_row = det_scale[0]
    in_weight = in_whole[0]
    out_weight = out_whole[0]

    def run_block(operand_tile):
        return detector_block(operand_tile, kernel, gain_row, in_weight, out_weight, scale_row)

    def skip_block(operand_tile):
        return jnp.zeros_like(operand_tile)

    def tick(tick_index, loop_state):
        incoming, finals = loop_state
        micro_num = tick_index - section_num
        is_valid = (micro_num >= 0) & (micro_num < micro_count)
        clipped = jnp.clip(micro_num, 0, micro_count - 1)
        fresh_tile = lax.dynamic_index_in_dim(tile_features, clipped, 0, keepdims=False)
        operand = jnp.where(section_num == 0, fresh_tile, incoming)
        result = lax.cond(is_valid, run_block, skip_block, operand)
        stored = lax.dynamic_update_index_in_dim(finals, result, clipped, 0)
        finals = jnp.where(is_valid & (section_num == sections - 1), stored, finals)
        incoming = passed_along(result, "section", 1)
        return (incoming, finals)

    start_state = (
        jnp.zeros(tile_features.shape[1:], jnp.bfloat16),
        jnp.zeros(tile_features.shape, jnp.bfloat16),
    )
    unused_tile, finals = lax.fori_loop(0, micro_count + sections - 1, tick, start_state)
    finals = spread(finals, "section", sections - 1)
    pixel_width = patches.shape[3]
    feat_width = finals.shape[3]
    full_width = cls_gain.shape[1]
    local_width = cls_embed.shape[1]
    local_heads = cls_qkv.shape[2] // HEAD_DIM
    qkv_flat = cls_qkv.reshape(cls_qkv.shape[0], -1)
    gain_first = lax.dynamic_slice_in_dim(cls_gain[0], section_num * local_width, local_width)
    slot_plan = crop_plan[0]
    source = lax.dynamic_index_in_dim(slot_from[0], section_num, 0, keepdims=False)
    zero_index = jnp.int32(0)

    def cut_crop(record):
        pixel_rows = lax.dynamic_slice(
            patches, (record[0], record[1], record[2], zero_index), (1, CROP, CROP, pixel_width)
        ).reshape(CROP * CROP, pixel_width)
        feat_rows = lax.dynamic_slice(
            finals, (record[0], record[1], record[2], zero_index), (1, CROP, CROP, feat_width)
        ).reshape(CROP * CROP, feat_width)
        return (pixel_rows, feat_rows)

    pixel_rows, feat_rows = jax.vmap(cut_crop)(slot_plan.reshape(-1, 3))
    count = pixel_rows.shape[0]
    widened = (
        jnp.einsum("crp,pd->crd", pixel_rows, cls_embed, preferred_element_type=jnp.float32)
        + jnp.einsum("crp,pd->crd", feat_rows, cls_merge, preferred_element_type=jnp.float32)
        + cls_pos.astype(jnp.float32)[None]
    )
    row_sum, row_square = lax.psum(
        (jnp.sum(widened, axis=-1), jnp.sum(widened * widened, axis=-1)), "section"
    )
    row_mean = row_sum / full_width
    row_var = row_square / full_width - row_mean * row_mean
    attn_part = (
        (widened - row_mean[..., None]) * lax.rsqrt(row_var[..., None] + epsilon) * gain_first
    ).astype(jnp.bfloat16)
    attn_in = lax.all_gather(attn_part, "section", axis=2, tiled=True)
    qkv = jnp.einsum("crd,de->cre", attn_in, qkv_flat, preferred_element_type=jnp.float32).astype(
        jnp.bfloat16
    )
    qkv = qkv.reshape(count, CROP * CROP, 3, local_heads, HEAD_DIM)
    query_rows = qkv[:, :, 0]
    key_rows = qkv[:, :, 1]
    value_rows = qkv[:, :, 2]
    scores = jnp.einsum(
        "cqhd,ckhd->chqk", query_rows, key_rows, preferred_element_type=jnp.float32
    ) * (1.0 / math.sqrt(HEAD_DIM))
    top_score = jnp.max(scores, axis=-1, keepdims=True)
    weights = jnp.exp(scores - top_score)
    probs = (weights / jnp.sum(weights, axis=-1, keepdims=True)).astype(jnp.bfloat16)
    context = jnp.einsum(
        "chqk,ckhd->cqhd", probs, value_rows, preferred_element_type=jnp.float32
    ).astype(jnp.bfloat16)
    context_mean = jnp.mean(context.reshape(count, CROP * CROP, -1).astype(jnp.float32), axis=1)
    context_term = jnp.dot(
        context_mean, cls_out.astype(jnp.float32), precision=lax.Precision.HIGHEST
    )
    token_mean = jnp.mean(widened, axis=1)
    placed = lax.dynamic_update_slice_in_dim(
        jnp.zeros((count, full_width), jnp.float32), token_mean, section_num * local_width, 1
    )
    terms = (placed + context_term).reshape(sections, -1)
    pooled = lax.psum_scatter(terms, "section", scatter_dimension=0, tiled=True).reshape(
        -1, full_width
    )
    results = layer_norm(pooled, cls_gain[1])
    outgoing_results = jnp.stack([results[0], results[2]], axis=0)
    extended_results = padded_2(outgoing_results, (("rep", 0),), 1)
    result = jnp.where(
        source == 1, extended_results[0], jnp.where(source == 3, extended_results[3], results[1])
    )
    result = jnp.where(source == 0, jnp.zeros_like(result), result)
    return result[None, None, :]


def solution(mesh):
    return jax.shard_map(
        per_device,
        mesh=mesh,
        in_specs=(
            P("rep", None, None, None),
            P("rep", None, None, None),
            P("section", None, None, None),
            P("section", None),
            P("section", None, "rep"),
            P("section", "rep", None),
            P("section", None),
            P(None, "section"),
            P(None, "section"),
            P(None, "section"),
            P(None, None, "section"),
            P("section", None),
            P(),
            P("rep", None, None, None),
            P("rep", None),
        ),
        out_specs=P("rep", "section", None),
        check_vma=False,
    )
```

profile of v0, /device:TPU:32, one launch (start us, length us, event | category | flops | bytes accessed | tf_op | source)
XLA Modules:
  0.0 480.8 jit_solution(15910834706224890067)
XLA Ops:
  8.1 0.8 copy.37
  9.0 0.9 copy.64
  9.9 52.1 %while.18 = (s32[]{:T(128)}, bf16[2,16,16,768]{3,2,1,0:T(8,128)(2,1)}, s32[12,4]{0,1:T(4,128)S(1)}, bf16[12,1,14,14,768]{4,3,2,1,0:T(8,128)(2,1)}, s32[]{:T(128)}) while((s32[]{:T(128)}, bf16[2,16,16,768]{3,2,1,0:T(8,128)(2,1)}, s32[12,4]{0,1:T(4,128)S(1)}, bf16[12,1,14,14,768]{4,3,2,1,0:T(8,128)(2,1)}, s32[]{:T(128)}) %tuple.126), condition=%wide.while_cond, body=%wide.while_body.sunk | while | flops 2 | bytes 690297 | solution.py:130
  10.6 3.7 bitcast_dynamic-update-slice_fusion.2
  14.9 3.7 bitcast_dynamic-update-slice_fusion.2
  19.2 3.7 bitcast_dynamic-update-slice_fusion.2
  23.6 3.7 bitcast_dynamic-update-slice_fusion.2
  27.9 3.7 bitcast_dynamic-update-slice_fusion.2
  32.3 3.7 bitcast_dynamic-update-slice_fusion.2
  36.6 3.7 bitcast_dynamic-update-slice_fusion.2
  41.0 3.7 bitcast_dynamic-update-slice_fusion.2
  45.3 3.7 bitcast_dynamic-update-slice_fusion.2
  49.6 3.7 bitcast_dynamic-update-slice_fusion.2
  54.0 3.7 bitcast_dynamic-update-slice_fusion.2
  58.3 3.7 bitcast_dynamic-update-slice_fusion.2
  62.0 34.7 %all-gather.4.cloned.1.call-done = bf16[1,512,2048]{1,2,0:T(8,128)(2,1)} async-done(((bf16[1,512,16]{1,2,0:T(8,128)(2,1)}), bf16[1,512,2048]{1,2,0:T(8,128)(2,1)}) %all-gather.4.cloned.1.call-update) | async-done | bytes 2097168 | tf_op jit(solution)/shard_map/all_gather | solution.py:84
  96.7 4.0 copy.39
  100.7 79.0 %all-gather.6.cloned.1.call-done = bf16[1,2048,512]{2,1,0:T(8,128)(2,1)} async-done(((bf16[1,16,512]{2,1,0:T(8,128)(2,1)}), bf16[1,2048,512]{2,1,0:T(8,128)(2,1)}) %all-gather.6.cloned.1.call-update) | async-done | bytes 2097168 | tf_op jit(solution)/shard_map/all_gather | solution.py:85
  179.7 84.6 %while.17 = (s32[]{:T(128)}, bf16[16,16,512]{2,1,0:T(8,128)(2,1)S(1)}, bf16[2,16,16,512]{3,2,1,0:T(8,128)(2,1)S(1)}, s32[]{:T(128)}, pred[]{:T(512)}, /*index=5*...) while((s32[]{:T(128)}, ...), condition=%wide.region_5.6_spmd, body=%wide.region_0.5_spmd.sunk | while | flops 1093009664 | bytes 12373336 | solution.py:116
  179.8 10.3 %conditional.2 = (bf16[16,16,512]{2,1,0:T(8,128)(2,1)}, bf16[1,16,16,512]{3,2,1,0:T(8,128)(2,1)S(1)}) conditional(s32[]{:T(128)} %convert_element_type.74, () %tuple.120, (pred[]{:T(512)}, bf16[2,16,16,512]{3,2,1,0:T(8,128)(2,1)S(1)}, s32[]{:T(128)}, bf16[16,16,512]{2,1,0:T(8,128)(2,1)S(1)}, f32[1,512]{1,0:T(1,128)S(1)}, ...), branch_computations={%region_1.1_spmd, %region_2.4_spmd} | conditional | flops 1092878592 | bytes 10538005 | solution.py:106
  180.0 4.2 fusion.129
  184.6 3.8 fusion.8
  188.4 0.8 add_convert_fusion
  189.2 0.9 copy.68
  190.1 1.3 collective-permute-start
  191.5 6.5 %collective-permute-done = bf16[16,16,512]{2,1,0:T(8,128)(2,1)S(1)} collective-permute-done((bf16[16,16,512]{2,1,0:T(8,128)(2,1)}, bf16[16,16,512]{2,1,0:T(8,128)(2,1)S(1)}, u32[]{:S(2)}, u32[]{:S(2)}) %collective-permute-start) | collective-permute-done | bytes 262176 | tf_op jit(solution)/shard_map/while/body/eval_jaxpr/ppermute | solution.py:16
  198.0 10.3 %conditional.2 = (bf16[16,16,512]{2,1,0:T(8,128)(2,1)}, bf16[1,16,16,512]{3,2,1,0:T(8,128)(2,1)S(1)}) conditional(s32[]{:T(128)} %convert_element_type.74, () %tuple.120, (pred[]{:T(512)}, bf16[2,16,16,512]{3,2,1,0:T(8,128)(2,1)S(1)}, s32[]{:T(128)}, bf16[16,16,512]{2,1,0:T(8,128)(2,1)S(1)}, f32[1,512]{1,0:T(1,128)S(1)}, ...), branch_computations={%region_1.1_spmd, %region_2.4_spmd} | conditional | flops 1092878592 | bytes 10538005 | solution.py:106
  198.1 4.2 fusion.129
  202.8 3.8 fusion.8
  206.6 0.8 add_convert_fusion
  207.4 0.9 copy.68
  208.3 4.3 collective-permute-start
  212.7 5.7 %collective-permute-done = bf16[16,16,512]{2,1,0:T(8,128)(2,1)S(1)} collective-permute-done((bf16[16,16,512]{2,1,0:T(8,128)(2,1)}, bf16[16,16,512]{2,1,0:T(8,128)(2,1)S(1)}, u32[]{:S(2)}, u32[]{:S(2)}) %collective-permute-start) | collective-permute-done | bytes 262176 | tf_op jit(solution)/shard_map/while/body/eval_jaxpr/ppermute | solution.py:16
  218.4 0.7 conditional.2
  218.4 0.7 broadcast.139
  219.2 13.9 %collective-permute-start = (bf16[16,16,512]{2,1,0:T(8,128)(2,1)}, bf16[16,16,512]{2,1,0:T(8,128)(2,1)S(1)}, u32[]{:S(2)}, u32[]{:S(2)}) collective-permute-start(bf16[16,16,512]{2,1,0:T(8,128)(2,1)} %get-tuple-element.531), channel_id=1, source_target_pairs={{0,128},{128,256},{256,384},{1,129},{129,257},{257,385},{2,130},{1... | collective-permute-start | bytes 786440 | tf_op jit(solution)/shard_map/while/body/eval_jaxpr/ppermute | solution.py:16
  233.1 4.8 %collective-permute-done = bf16[16,16,512]{2,1,0:T(8,128)(2,1)S(1)} collective-permute-done((bf16[16,16,512]{2,1,0:T(8,128)(2,1)}, bf16[16,16,512]{2,1,0:T(8,128)(2,1)S(1)}, u32[]{:S(2)}, u32[]{:S(2)}) %collective-permute-start) | collective-permute-done | bytes 262176 | tf_op jit(solution)/shard_map/while/body/eval_jaxpr/ppermute | solution.py:16
  237.9 0.7 conditional.2
  237.9 0.7 broadcast.139
  238.7 4.3 collective-permute-start
  243.1 4.1 collective-permute-done
  247.2 0.7 conditional.2
  247.2 0.7 broadcast.139
  247.9 12.2 %collective-permute-start = (bf16[16,16,512]{2,1,0:T(8,128)(2,1)}, bf16[16,16,512]{2,1,0:T(8,128)(2,1)S(1)}, u32[]{:S(2)}, u32[]{:S(2)}) collective-permute-start(bf16[16,16,512]{2,1,0:T(8,128)(2,1)} %get-tuple-element.531), channel_id=1, source_target_pairs={{0,128},{128,256},{256,384},{1,129},{129,257},{257,385},{2,130},{1... | collective-permute-start | bytes 786440 | tf_op jit(solution)/shard_map/while/body/eval_jaxpr/ppermute | solution.py:16
  260.2 4.1 collective-permute-done
  264.3 1.5 broadcast_select_fusion
  266.1 6.0 %reshape.115 = bf16[12,196,768]{2,1,0:T(8,128)(2,1)} reshape(bf16[12,1,14,14,768]{4,3,2,1,0:T(8,128)(2,1)} %get-tuple-element.289) | data formatting | bytes 7225344 | tf_op jit(solution)/shard_map/vmap()/reshape | solution.py:132
  272.2 3.2 fusion.123
  275.3 52.9 %all-reduce.5.cloned.1.call-done = bf16[2,16,16,512]{3,0,2,1:T(2,128)(2,1)} async-done(((bf16[2,16,16,512]{3,0,2,1:T(2,128)(2,1)}), bf16[2,16,16,512]{3,0,2,1:T(2,128)(2,1)}) %all-reduce.5.cloned.1.call-update) | async-done | bytes 524304 | tf_op jit(solution)/shard_map/psum | solution.py:21
  328.2 12.1 %gather_fusion = bf16[12,14,14,512]{3,0,2,1:T(8,128)(2,1)} fusion(bf16[2,16,16,512]{3,0,2,1:T(2,128)(2,1)} %all-reduce.5.cloned.1.call-done, s32[12]{0:T(128)S(1)} %get-tuple-element.423), kind=kCustom, calls=%fused_computation | custom fusion | bytes 4817088 | tf_op jit(solution)/shard_map/vmap()/gather | solution.py:133
  340.3 6.5 %fusion.128 = (f32[12,256]{1,0:T(8,128)S(1)}, f32[12,196]{1,0:T(8,128)S(1)}, f32[12,196]{1,0:T(8,128)S(1)}, f32[12,196,256]{2,1,0:T(8,128)}) fusion(f32[196,256]{1,0:T(8,128)S(1)} %convert_element_type.50, f32[12,196,256]{2,1,0:T(8,128)S(1)} %fusion.123, bf16[512,256]{1,0:T(8,128)(2,1)S(1)} %copy-done.9, bf16[12,196,512]{2,0,1:T(8,128)(2,1)} %bitcast.131), kind=kOutput, calls=%fused_computation.214 | convolution fusion | flops 620167552 | bytes 7719296 | tf_op jit(solution)/shard_map/crp,pd->crd/dot_general | solution.py:142
  346.7 16.1 %all-reduce.2 = (f32[12,196]{1,0:T(8,128)S(1)}, f32[12,196]{1,0:T(8,128)S(1)}) all-reduce(f32[12,196]{1,0:T(8,128)S(1)} %get-tuple-element.327, f32[12,196]{1,0:T(8,128)S(1)} %get-tuple-element.328), channel_id=1, replica_groups=mesh['section'=4,'rep'=128] {'section'}, use_global_device_ids=true, to_apply=%region_10.11 | all-reduce | flops 4704 | bytes 37632 | tf_op jit(solution)/shard_map/psum | solution.py:145
  362.8 3.0 multiply_convert_fusion.1
  366.2 1.3 dynamic-slice.12
  367.5 61.6 %all-gather.8.cloned.1.call-done = bf16[12,196,1024]{2,1,0:T(8,128)(2,1)} async-done(((bf16[12,196,256]{2,1,0:T(8,128)(2,1)}), bf16[12,196,1024]{2,1,0:T(8,128)(2,1)}) %all-gather.8.cloned.1.call-update) | async-done | bytes 4816912 | tf_op jit(solution)/shard_map/all_gather | solution.py:153
  429.1 6.4 %convolution_convert_fusion = bf16[12,196,384]{2,1,0:T(8,128)(2,1)} fusion(bf16[12,196,1024]{2,1,0:T(8,128)(2,1)} %all-gather.8.cloned.1.call-done, bf16[1024,384,1]{0,1,2:T(8,128)(2,1)S(1)} %bitcast.133), kind=kOutput, calls=%fused_computation.181 | convolution fusion | flops 1850591232 | bytes 7409664 | tf_op jit(solution)/shard_map/crd,de->cre/dot_general | solution.py:154
  435.6 2.7 copy.44
  438.3 0.8 fusion.122
  439.1 4.1 fusion.137
  443.3 0.8 convert_reduce_fusion
  444.5 16.7 %all-reduce.1 = f32[4,3072]{1,0:T(4,128)S(1)} all-reduce(f32[4,3072]{1,0:T(4,128)S(1)} %reshape.119), channel_id=2, replica_groups=mesh['section'=4,'rep'=128] {'section'}, use_global_device_ids=true, to_apply=%region_15.16.clone | all-reduce | flops 12288 | bytes 98304
  462.3 1.9 collective-permute-start.1
  464.3 7.0 %collective-permute-start.2 = (f32[1,1024]{1,0:T(1,128)S(1)}, f32[1,1024]{1,0:T(1,128)S(1)}, u32[]{:S(2)}, u32[]{:S(2)}) collective-permute-start(f32[1,1024]{1,0:T(1,128)S(1)} %get-tuple-element.417), channel_id=1, source_target_pairs={{1,0},{2,1},{3,2},{4,3},{5,4},{6,5},{7,6},{8,7},{9,8},{10,9},{11,1... | collective-permute-start | bytes 12296 | tf_op jit(solution)/shard_map/ppermute | solution.py:32
  473.1 1.2 fusion.126
  (104 shorter events, 14.0 us)
Async XLA Ops:
  6.5 265.6 %copy-start = (bf16[768,256]{1,0:T(8,128)(2,1)S(1)}, bf16[768,256]{1,0:T(8,128)(2,1)}, u32[]{:S(2)}) copy-start(bf16[768,256]{1,0:T(8,128)(2,1)} %param.26) | copy-start | bytes 1179652
  6.5 90.1 %all-gather.4.cloned.1.call-start = ((), (), s32[]{:S(2)}) async-start(), calls=%async_computation | async-start | bytes 2113536 | tf_op jit(solution)/shard_map/all_gather | solution.py:84
  7.3 172.4 %all-gather.6.cloned.1.call-start = ((), (), s32[]{:S(2)}) async-start(), calls=%async_computation.1 | async-start | bytes 2113536 | tf_op jit(solution)/shard_map/all_gather | solution.py:85
  8.0 320.2 %all-reduce.5.cloned.1.call-start = ((), (), s32[]{:S(2)}) async-start(), calls=%async_computation.2 | async-start | bytes 1048576 | tf_op jit(solution)/shard_map/psum | solution.py:21
  96.7 83.1 %copy-start.1 = (bf16[2,16,16,512]{3,2,1,0:T(8,128)(2,1)S(1)}, bf16[2,16,16,512]{3,2,1,0:T(8,128)(2,1)}, u32[]{:S(2)}) copy-start(bf16[2,16,16,512]{3,2,1,0:T(8,128)(2,1)} %param.19) | copy-start | bytes 1572868
  96.7 83.1 %copy-start.5 = (f32[1,512]{1,0:T(1,128)S(1)}, f32[1,512]{1,0:T(1,128)}, u32[]{:S(2)}) copy-start(f32[1,512]{1,0:T(1,128)} %param.25) | copy-start | bytes 6148
  96.7 83.1 %copy-start.6 = (f32[1,512]{1,0:T(1,128)S(1)}, f32[1,512]{1,0:T(1,128)}, u32[]{:S(2)}) copy-start(f32[1,512]{1,0:T(1,128)} %param.22) | copy-start | bytes 6148
  179.7 86.3 %copy-start.7 = (f32[2,1024]{1,0:T(2,128)S(1)}, f32[2,1024]{1,0:T(2,128)}, u32[]{:S(2)}) copy-start(f32[2,1024]{1,0:T(2,128)} %param.31) | copy-start | bytes 24580
  190.1 7.9 %collective-permute-start = (bf16[16,16,512]{2,1,0:T(8,128)(2,1)}, bf16[16,16,512]{2,1,0:T(8,128)(2,1)S(1)}, u32[]{:S(2)}, u32[]{:S(2)}) collective-permute-start(bf16[16,16,512]{2,1,0:T(8,128)(2,1)} %get-tuple-element.531), channel_id=1, source_target_pairs={{0,128},{128,256},{256,384},{1,129},{129,257},{257,385},{2,130},{1... | collective-permute-start | bytes 786440 | tf_op jit(solution)/shard_map/while/body/eval_jaxpr/ppermute | solution.py:16
  208.3 10.1 %collective-permute-start = (bf16[16,16,512]{2,1,0:T(8,128)(2,1)}, bf16[16,16,512]{2,1,0:T(8,128)(2,1)S(1)}, u32[]{:S(2)}, u32[]{:S(2)}) collective-permute-start(bf16[16,16,512]{2,1,0:T(8,128)(2,1)} %get-tuple-element.531), channel_id=1, source_target_pairs={{0,128},{128,256},{256,384},{1,129},{129,257},{257,385},{2,130},{1... | collective-permute-start | bytes 786440 | tf_op jit(solution)/shard_map/while/body/eval_jaxpr/ppermute | solution.py:16
  219.2 18.8 %collective-permute-start = (bf16[16,16,512]{2,1,0:T(8,128)(2,1)}, bf16[16,16,512]{2,1,0:T(8,128)(2,1)S(1)}, u32[]{:S(2)}, u32[]{:S(2)}) collective-permute-start(bf16[16,16,512]{2,1,0:T(8,128)(2,1)} %get-tuple-element.531), channel_id=1, source_target_pairs={{0,128},{128,256},{256,384},{1,129},{129,257},{257,385},{2,130},{1... | collective-permute-start | bytes 786440 | tf_op jit(solution)/shard_map/while/body/eval_jaxpr/ppermute | solution.py:16
  238.7 8.5 %collective-permute-start = (bf16[16,16,512]{2,1,0:T(8,128)(2,1)}, bf16[16,16,512]{2,1,0:T(8,128)(2,1)S(1)}, u32[]{:S(2)}, u32[]{:S(2)}) collective-permute-start(bf16[16,16,512]{2,1,0:T(8,128)(2,1)} %get-tuple-element.531), channel_id=1, source_target_pairs={{0,128},{128,256},{256,384},{1,129},{129,257},{257,385},{2,130},{1... | collective-permute-start | bytes 786440 | tf_op jit(solution)/shard_map/while/body/eval_jaxpr/ppermute | solution.py:16
  247.9 16.4 %collective-permute-start = (bf16[16,16,512]{2,1,0:T(8,128)(2,1)}, bf16[16,16,512]{2,1,0:T(8,128)(2,1)S(1)}, u32[]{:S(2)}, u32[]{:S(2)}) collective-permute-start(bf16[16,16,512]{2,1,0:T(8,128)(2,1)} %get-tuple-element.531), channel_id=1, source_target_pairs={{0,128},{128,256},{256,384},{1,129},{129,257},{257,385},{2,130},{1... | collective-permute-start | bytes 786440 | tf_op jit(solution)/shard_map/while/body/eval_jaxpr/ppermute | solution.py:16
  265.8 163.3 %all-gather.8.cloned.1.call-start = ((), (), s32[]{:S(2)}) async-start(), calls=%async_computation.3 | async-start | bytes 6144000 | tf_op jit(solution)/shard_map/all_gather | solution.py:153
  266.1 6.0 %copy-start.4 = (bf16[196,256]{1,0:T(8,128)(2,1)S(1)}, bf16[196,256]{1,0:T(8,128)(2,1)}, u32[]{:S(2)}) copy-start(bf16[196,256]{1,0:T(8,128)(2,1)} %param.28) | copy-start | bytes 301060
  328.2 12.1 %copy-start.9 = (bf16[512,256]{1,0:T(8,128)(2,1)S(1)}, bf16[512,256]{1,0:T(8,128)(2,1)}, u32[]{:S(2)}) copy-start(bf16[512,256]{1,0:T(8,128)(2,1)} %param.27) | copy-start | bytes 786436
  362.8 3.1 copy-start.2
  443.3 1.0 copy-start.3
  443.3 28.0 %copy-start.8 = (s32[1,4]{1,0:T(1,128)S(1)}, s32[1,4]{1,0:T(1,128)}, u32[]{:S(2)}) copy-start(s32[1,4]{1,0:T(1,128)} %param.33) | copy-start | bytes 52
  462.3 10.8 %collective-permute-start.1 = (f32[1,1024]{1,0:T(1,128)S(1)}, f32[1,1024]{1,0:T(1,128)S(1)}, u32[]{:S(2)}, u32[]{:S(2)}) collective-permute-start(f32[1,1024]{1,0:T(1,128)S(1)} %get-tuple-element.418), channel_id=1, source_target_pairs={{0,1},{1,2},{2,3},{3,4},{4,5},{5,6},{6,7},{7,8},{8,9},{9,10},{10,1... | collective-permute-start | bytes 12296 | tf_op jit(solution)/shard_map/ppermute | solution.py:29
  464.3 8.9 %collective-permute-start.2 = (f32[1,1024]{1,0:T(1,128)S(1)}, f32[1,1024]{1,0:T(1,128)S(1)}, u32[]{:S(2)}, u32[]{:S(2)}) collective-permute-start(f32[1,1024]{1,0:T(1,128)S(1)} %get-tuple-element.417), channel_id=1, source_target_pairs={{1,0},{2,1},{3,2},{4,3},{5,4},{6,5},{7,6},{8,7},{9,8},{10,9},{11,1... | collective-permute-start | bytes 12296 | tf_op jit(solution)/shard_map/ppermute | solution.py:32
Sparse Core Ops, SparseCore 0:
  10.5 86.1 all-gather.3
  99.8 79.7 all-gather.5
  265.9 62.2 all-reduce.4
  366.0 63.1 all-gather.7
where the time goes:
time: 482 us; the launch traced here: 481 us
  waiting for transfers between devices  255 us (53%)
  local copies, waits for them, and re-layouts  85.6 us (18%)
  starting transfers between devices  45.1 us (9%)
  blocking collectives  32.7 us (7%)
  matrix products  25.5 us (5%)
  other arithmetic  22.2 us (5%)
  between operations  14.8 us (3%)
    all_gather x1, waiting for transfers between devices, per_device(): lax.all_gather(det_out, 'rep', axis=1, tiled=True)  79 us
    all_gather x1, waiting for transfers between devices, per_device(): attn_in = lax.all_gather(attn_part, 'section', axis=2, tiled=True)  61.6 us
    psum x1, waiting for transfers between devices, spread(): return lax.psum(kept, axis)  52.9 us
    gather x36, local copies, waits for them, and re-layouts  52 us
    ppermute x5, starting transfers between devices, passed_along(): return lax.ppermute(block, axis, route)  35.9 us
    all_gather x1, waiting for transfers between devices, per_device(): lax.all_gather(det_in, 'rep', axis=2, tiled=True)  34.7 us
    ppermute x5, waiting for transfers between devices, passed_along(): return lax.ppermute(block, axis, route)  25.1 us
    unnamed x1, blocking collectives  16.7 us
  transfers between devices with their start and end apart: 11, of which 9 were waited for; matrix products, arithmetic and copies ran while one was open for 15% of the time, Pallas kernels for 0%

commit v1 on v0

--- a/solution.py
+++ b/solution.py
@@ -10,6 +10,10 @@
 epsilon = 1e-06
 
 
+def take_zones(state, axis_key):
+    return jnp.sum(lax.all_gather(state, axis_name=axis_key), axis=0)
+
+
 def passed_along(block, axis, distance):
     devices = range(lax.axis_size(axis))
     route = [(i - distance, i) for i in devices if i - distance in devices]
@@ -18,7 +22,7 @@
 
 def spread(value, axis, source):
     kept = jnp.where(lax.axis_index(axis) == source, value, 0).astype(value.dtype)
-    return lax.psum(kept, axis)
+    return take_zones(kept, axis)
 
 
 def padded_2(block, sides, width):

time: 482 us -> 491 us (1.019)
  blocking collectives: 32.7 us -> 44.4 us
  waiting for transfers between devices: 255 us -> 250 us
    psum x1 -> x0, waiting for transfers between devices: 52.9 us -> none  [spread(): return lax.psum(kept, axis)]
    all_gather x1, waiting for transfers between devices: 34.7 us -> 86.7 us  [per_device(): lax.all_gather(det_in, 'rep', axis=2, tiled=True)]
    psum x1, blocking collectives: 16.1 us -> 27.8 us  [per_device(): lax.psum((jnp.sum(widened, axis=-1), jnp.sum(widened * widened, axis=-1))...]
  transfers between devices with their start and end apart: 11 -> 11, of which waited for: 9 -> 8; matrix products, arithmetic and copies ran while one was open for 15% -> 15% of each run, Pallas kernels for 0% -> 0%
where the time goes in v1:
time: 491 us; the launch traced here: 489 us
  waiting for transfers between devices  250 us (51%)
  local copies, waits for them, and re-layouts  83.2 us (17%)
  starting transfers between devices  45.2 us (9%)
  blocking collectives  44.4 us (9%)
  matrix products  25.5 us (5%)
  other arithmetic  25.4 us (5%)
  between operations  14.7 us (3%)
    all_gather x1, waiting for transfers between devices, per_device(): lax.all_gather(det_in, 'rep', axis=2, tiled=True)  86.7 us
    all_gather x1, waiting for transfers between devices, per_device(): lax.all_gather(det_out, 'rep', axis=1, tiled=True)  78.9 us
    all_gather x1, waiting for transfers between devices, per_device(): attn_in = lax.all_gather(attn_part, 'section', axis=2, tiled=True)  58.4 us
    gather x36, local copies, waits for them, and re-layouts  52.6 us
    ppermute x5, starting transfers between devices, passed_along(): return lax.ppermute(block, axis, route)  36 us
    psum x1, blocking collectives, per_device(): lax.psum((jnp.sum(widened, axis=-1), jnp.sum(widened * widened, axis=-1))...  27.8 us
    ppermute x5, waiting for transfers between devices, passed_along(): return lax.ppermute(block, axis, route)  25.1 us
    unnamed x1, blocking collectives  16.7 us
  transfers between devices with their start and end apart: 11, of which 8 were waited for; matrix products, arithmetic and copies ran while one was open for 15% of the time, Pallas kernels for 0%

profile of v1, /device:TPU:32, one launch (start us, length us, event | category | flops | bytes accessed | tf_op | source)
XLA Modules:
  0.0 489.2 jit_solution(17423052550032170355)
XLA Ops:
  8.1 0.9 copy.58
  9.0 0.8 copy.33
  9.9 86.7 %all-gather.6.cloned.1.call-done = bf16[1,512,2048]{1,2,0:T(8,128)(2,1)} async-done(((bf16[1,512,16]{1,2,0:T(8,128)(2,1)}), bf16[1,512,2048]{1,2,0:T(8,128)(2,1)}) %all-gather.6.cloned.1.call-update) | async-done | bytes 2097168 | tf_op jit(solution)/shard_map/all_gather | solution.py:88
  96.6 4.1 copy.34
  100.6 78.9 %all-gather.8.cloned.1.call-done = bf16[1,2048,512]{2,1,0:T(8,128)(2,1)} async-done(((bf16[1,16,512]{2,1,0:T(8,128)(2,1)}), bf16[1,2048,512]{2,1,0:T(8,128)(2,1)}) %all-gather.8.cloned.1.call-update) | async-done | bytes 2097168 | tf_op jit(solution)/shard_map/all_gather | solution.py:89
  179.7 84.6 %while.17 = (s32[]{:T(128)}, bf16[16,16,512]{2,1,0:T(8,128)(2,1)S(1)}, bf16[2,16,16,512]{3,2,1,0:T(8,128)(2,1)S(1)}, s32[]{:T(128)}, pred[]{:T(512)}, /*index=5*...) while((s32[]{:T(128)}, ...), condition=%wide.region_5.6_spmd, body=%wide.region_0.5_spmd.sunk | while | flops 1093009664 | bytes 12373336 | solution.py:120
  179.7 10.4 %conditional.2 = (bf16[16,16,512]{2,1,0:T(8,128)(2,1)}, bf16[1,16,16,512]{3,2,1,0:T(8,128)(2,1)S(1)}) conditional(s32[]{:T(128)} %convert_element_type.76, () %tuple.118, (pred[]{:T(512)}, bf16[2,16,16,512]{3,2,1,0:T(8,128)(2,1)S(1)}, s32[]{:T(128)}, bf16[16,16,512]{2,1,0:T(8,128)(2,1)S(1)}, f32[1,512]{1,0:T(1,128)S(1)}, ...), branch_computations={%region_1.1_spmd, %region_2.4_spmd} | conditional | flops 1092878592 | bytes 10538005 | solution.py:110
  179.9 4.2 fusion.129
  184.5 3.8 fusion.8
  188.3 0.8 add_convert_fusion
  189.1 0.9 copy.62
  190.0 1.3 collective-permute-start
  191.4 6.5 %collective-permute-done = bf16[16,16,512]{2,1,0:T(8,128)(2,1)S(1)} collective-permute-done((bf16[16,16,512]{2,1,0:T(8,128)(2,1)}, bf16[16,16,512]{2,1,0:T(8,128)(2,1)S(1)}, u32[]{:S(2)}, u32[]{:S(2)}) %collective-permute-start) | collective-permute-done | bytes 262176 | tf_op jit(solution)/shard_map/while/body/eval_jaxpr/ppermute | solution.py:20
  197.9 10.3 %conditional.2 = (bf16[16,16,512]{2,1,0:T(8,128)(2,1)}, bf16[1,16,16,512]{3,2,1,0:T(8,128)(2,1)S(1)}) conditional(s32[]{:T(128)} %convert_element_type.76, () %tuple.118, (pred[]{:T(512)}, bf16[2,16,16,512]{3,2,1,0:T(8,128)(2,1)S(1)}, s32[]{:T(128)}, bf16[16,16,512]{2,1,0:T(8,128)(2,1)S(1)}, f32[1,512]{1,0:T(1,128)S(1)}, ...), branch_computations={%region_1.1_spmd, %region_2.4_spmd} | conditional | flops 1092878592 | bytes 10538005 | solution.py:110
  198.1 4.2 fusion.129
  202.7 3.8 fusion.8
  206.5 0.8 add_convert_fusion
  207.3 0.9 copy.62
  208.2 4.3 collective-permute-start
  212.6 5.7 %collective-permute-done = bf16[16,16,512]{2,1,0:T(8,128)(2,1)S(1)} collective-permute-done((bf16[16,16,512]{2,1,0:T(8,128)(2,1)}, bf16[16,16,512]{2,1,0:T(8,128)(2,1)S(1)}, u32[]{:S(2)}, u32[]{:S(2)}) %collective-permute-start) | collective-permute-done | bytes 262176 | tf_op jit(solution)/shard_map/while/body/eval_jaxpr/ppermute | solution.py:20
  218.3 0.8 conditional.2
  218.3 0.7 broadcast.139
  219.1 13.8 %collective-permute-start = (bf16[16,16,512]{2,1,0:T(8,128)(2,1)}, bf16[16,16,512]{2,1,0:T(8,128)(2,1)S(1)}, u32[]{:S(2)}, u32[]{:S(2)}) collective-permute-start(bf16[16,16,512]{2,1,0:T(8,128)(2,1)} %get-tuple-element.507), channel_id=1, source_target_pairs={{0,128},{128,256},{256,384},{1,129},{129,257},{257,385},{2,130},{1... | collective-permute-start | bytes 786440 | tf_op jit(solution)/shard_map/while/body/eval_jaxpr/ppermute | solution.py:20
  233.0 4.8 collective-permute-done
  237.8 0.8 conditional.2
  237.8 0.7 broadcast.139
  238.6 4.3 collective-permute-start
  243.0 4.1 collective-permute-done
  247.1 0.8 conditional.2
  247.9 12.2 %collective-permute-start = (bf16[16,16,512]{2,1,0:T(8,128)(2,1)}, bf16[16,16,512]{2,1,0:T(8,128)(2,1)S(1)}, u32[]{:S(2)}, u32[]{:S(2)}) collective-permute-start(bf16[16,16,512]{2,1,0:T(8,128)(2,1)} %get-tuple-element.507), channel_id=1, source_target_pairs={{0,128},{128,256},{256,384},{1,129},{129,257},{257,385},{2,130},{1... | collective-permute-start | bytes 786440 | tf_op jit(solution)/shard_map/while/body/eval_jaxpr/ppermute | solution.py:20
  260.2 4.1 collective-permute-done
  264.3 0.9 broadcast_select_fusion
  265.4 52.6 %while.18 = (s32[]{:T(128)}, bf16[2,16,16,768]{3,2,1,0:T(8,128)(2,1)}, s32[12,4]{0,1:T(4,128)S(1)}, bf16[12,1,14,14,768]{4,3,2,1,0:T(8,128)(2,1)}, s32[]{:T(128)}) while((s32[]{:T(128)}, bf16[2,16,16,768]{3,2,1,0:T(8,128)(2,1)}, s32[12,4]{0,1:T(4,128)S(1)}, bf16[12,1,14,14,768]{4,3,2,1,0:T(8,128)(2,1)}, s32[]{:T(128)}) %tuple.124), condition=%wide.while_cond, body=%wide.while_body.sunk | while | flops 2 | bytes 690297 | solution.py:134
  266.1 3.7 bitcast_dynamic-update-slice_fusion.2
  270.4 3.7 bitcast_dynamic-update-slice_fusion.2
  274.8 3.7 bitcast_dynamic-update-slice_fusion.2
  279.2 3.7 bitcast_dynamic-update-slice_fusion.2
  283.6 3.7 bitcast_dynamic-update-slice_fusion.2
  288.0 3.7 bitcast_dynamic-update-slice_fusion.2
  292.4 3.7 bitcast_dynamic-update-slice_fusion.2
  296.8 3.7 bitcast_dynamic-update-slice_fusion.2
  301.1 3.7 bitcast_dynamic-update-slice_fusion.2
  305.5 3.7 bitcast_dynamic-update-slice_fusion.2
  309.9 3.7 bitcast_dynamic-update-slice_fusion.2
  314.3 3.7 bitcast_dynamic-update-slice_fusion.2
  318.0 6.0 %reshape.115 = bf16[12,196,768]{2,1,0:T(8,128)(2,1)} reshape(bf16[12,1,14,14,768]{4,3,2,1,0:T(8,128)(2,1)} %get-tuple-element.289) | data formatting | bytes 7225344 | tf_op jit(solution)/shard_map/vmap()/reshape | solution.py:136
  324.8 3.2 fusion.123
  328.0 2.9 reduce_sum.95
  330.9 1.6 copy.35
  332.5 7.4 %gather_fusion = bf16[12,14,14,512]{3,0,2,1:T(8,128)(2,1)} fusion(bf16[2,16,16,512]{3,0,2,1:T(2,128)(2,1)S(1)} %copy.35, s32[12]{0:T(128)S(1)} %get-tuple-element.399), kind=kCustom, calls=%fused_computation | custom fusion | bytes 4817088 | tf_op jit(solution)/shard_map/vmap()/gather | solution.py:137
  339.9 6.5 %fusion.128 = (f32[12,256]{1,0:T(8,128)S(1)}, f32[12,196]{1,0:T(8,128)S(1)}, f32[12,196]{1,0:T(8,128)S(1)}, f32[12,196,256]{2,1,0:T(8,128)}) fusion(f32[196,256]{1,0:T(8,128)} %convert_element_type.52, f32[12,196,256]{2,1,0:T(8,128)S(1)} %fusion.123, bf16[512,256]{1,0:T(8,128)(2,1)} %param.27, bf16[12,196,512]{2,0,1:T(8,128)(2,1)} %bitcast.132), kind=kOutput, calls=%fused_computation.214 | convolution fusion | flops 620167552 | bytes 7719296 | tf_op jit(solution)/shard_map/crp,pd->crd/dot_general | solution.py:146
  346.4 27.8 %all-reduce.2 = (f32[12,196]{1,0:T(8,128)S(1)}, f32[12,196]{1,0:T(8,128)S(1)}) all-reduce(f32[12,196]{1,0:T(8,128)S(1)} %get-tuple-element.303, f32[12,196]{1,0:T(8,128)S(1)} %get-tuple-element.304), channel_id=1, replica_groups=mesh['section'=4,'rep'=128] {'section'}, use_global_device_ids=true, to_apply=%region_10.11 | all-reduce | flops 4704 | bytes 37632 | tf_op jit(solution)/shard_map/psum | solution.py:149
  374.2 3.0 multiply_convert_fusion.1
  377.6 1.3 dynamic-slice.12
  378.9 58.4 %all-gather.10.cloned.1.call-done = bf16[12,196,1024]{2,1,0:T(8,128)(2,1)} async-done(((bf16[12,196,256]{2,1,0:T(8,128)(2,1)}), bf16[12,196,1024]{2,1,0:T(8,128)(2,1)}) %all-gather.10.cloned.1.call-update) | async-done | bytes 4816912 | tf_op jit(solution)/shard_map/all_gather | solution.py:157
  437.3 6.4 %convolution_convert_fusion = bf16[12,196,384]{2,1,0:T(8,128)(2,1)} fusion(bf16[12,196,1024]{2,1,0:T(8,128)(2,1)} %all-gather.10.cloned.1.call-done, bf16[1024,384,1]{0,1,2:T(8,128)(2,1)S(1)} %bitcast.135), kind=kOutput, calls=%fused_computation.181 | convolution fusion | flops 1850591232 | bytes 7409664 | tf_op jit(solution)/shard_map/crd,de->cre/dot_general | solution.py:158
  443.7 2.7 copy.39
  446.4 0.8 fusion.122
  447.3 4.1 fusion.137
  451.5 0.8 convert_reduce_fusion
  452.7 16.7 %all-reduce.1 = f32[4,3072]{1,0:T(4,128)S(1)} all-reduce(f32[4,3072]{1,0:T(4,128)S(1)} %reshape.119), channel_id=3, replica_groups=mesh['section'=4,'rep'=128] {'section'}, use_global_device_ids=true, to_apply=%region_15.16.clone | all-reduce | flops 12288 | bytes 98304
  470.5 1.9 collective-permute-start.1
  472.4 7.0 %collective-permute-start.2 = (f32[1,1024]{1,0:T(1,128)S(1)}, f32[1,1024]{1,0:T(1,128)S(1)}, u32[]{:S(2)}, u32[]{:S(2)}) collective-permute-start(f32[1,1024]{1,0:T(1,128)S(1)} %get-tuple-element.393), channel_id=1, source_target_pairs={{1,0},{2,1},{3,2},{4,3},{5,4},{6,5},{7,6},{8,7},{9,8},{10,9},{11,1... | collective-permute-start | bytes 12296 | tf_op jit(solution)/shard_map/ppermute | solution.py:36
  481.4 1.3 fusion.126
  (104 shorter events, 15.4 us)
Async XLA Ops:
  6.5 318.2 %copy-start = (bf16[768,256]{1,0:T(8,128)(2,1)S(1)}, bf16[768,256]{1,0:T(8,128)(2,1)}, u32[]{:S(2)}) copy-start(bf16[768,256]{1,0:T(8,128)(2,1)} %param.26) | copy-start | bytes 1179652
  6.5 90.0 %all-gather.6.cloned.1.call-start = ((), (), s32[]{:S(2)}) async-start(), calls=%async_computation | async-start | bytes 2113536 | tf_op jit(solution)/shard_map/all_gather | solution.py:88
  7.3 172.3 %all-gather.8.cloned.1.call-start = ((), (), s32[]{:S(2)}) async-start(), calls=%async_computation.1 | async-start | bytes 2113536 | tf_op jit(solution)/shard_map/all_gather | solution.py:89
  8.0 320.0 %all-gather.12.cloned.1.call-start = ((), (), s32[]{:S(2)}) async-start(), calls=%async_computation.3 | async-start | bytes 2621440 | tf_op jit(solution)/shard_map/all_gather | solution.py:14
  96.6 83.1 %copy-start.1 = (bf16[2,16,16,512]{3,2,1,0:T(8,128)(2,1)S(1)}, bf16[2,16,16,512]{3,2,1,0:T(8,128)(2,1)}, u32[]{:S(2)}) copy-start(bf16[2,16,16,512]{3,2,1,0:T(8,128)(2,1)} %param.19) | copy-start | bytes 1572868
  96.6 83.1 %copy-start.5 = (f32[1,512]{1,0:T(1,128)S(1)}, f32[1,512]{1,0:T(1,128)}, u32[]{:S(2)}) copy-start(f32[1,512]{1,0:T(1,128)} %param.25) | copy-start | bytes 6148
  96.6 83.1 %copy-start.6 = (f32[1,512]{1,0:T(1,128)S(1)}, f32[1,512]{1,0:T(1,128)}, u32[]{:S(2)}) copy-start(f32[1,512]{1,0:T(1,128)} %param.22) | copy-start | bytes 6148
  190.0 7.9 %collective-permute-start = (bf16[16,16,512]{2,1,0:T(8,128)(2,1)}, bf16[16,16,512]{2,1,0:T(8,128)(2,1)S(1)}, u32[]{:S(2)}, u32[]{:S(2)}) collective-permute-start(bf16[16,16,512]{2,1,0:T(8,128)(2,1)} %get-tuple-element.507), channel_id=1, source_target_pairs={{0,128},{128,256},{256,384},{1,129},{129,257},{257,385},{2,130},{1... | collective-permute-start | bytes 786440 | tf_op jit(solution)/shard_map/while/body/eval_jaxpr/ppermute | solution.py:20
  208.2 10.1 %collective-permute-start = (bf16[16,16,512]{2,1,0:T(8,128)(2,1)}, bf16[16,16,512]{2,1,0:T(8,128)(2,1)S(1)}, u32[]{:S(2)}, u32[]{:S(2)}) collective-permute-start(bf16[16,16,512]{2,1,0:T(8,128)(2,1)} %get-tuple-element.507), channel_id=1, source_target_pairs={{0,128},{128,256},{256,384},{1,129},{129,257},{257,385},{2,130},{1... | collective-permute-start | bytes 786440 | tf_op jit(solution)/shard_map/while/body/eval_jaxpr/ppermute | solution.py:20
  219.1 18.7 %collective-permute-start = (bf16[16,16,512]{2,1,0:T(8,128)(2,1)}, bf16[16,16,512]{2,1,0:T(8,128)(2,1)S(1)}, u32[]{:S(2)}, u32[]{:S(2)}) collective-permute-start(bf16[16,16,512]{2,1,0:T(8,128)(2,1)} %get-tuple-element.507), channel_id=1, source_target_pairs={{0,128},{128,256},{256,384},{1,129},{129,257},{257,385},{2,130},{1... | collective-permute-start | bytes 786440 | tf_op jit(solution)/shard_map/while/body/eval_jaxpr/ppermute | solution.py:20
  238.6 8.5 %collective-permute-start = (bf16[16,16,512]{2,1,0:T(8,128)(2,1)}, bf16[16,16,512]{2,1,0:T(8,128)(2,1)S(1)}, u32[]{:S(2)}, u32[]{:S(2)}) collective-permute-start(bf16[16,16,512]{2,1,0:T(8,128)(2,1)} %get-tuple-element.507), channel_id=1, source_target_pairs={{0,128},{128,256},{256,384},{1,129},{129,257},{257,385},{2,130},{1... | collective-permute-start | bytes 786440 | tf_op jit(solution)/shard_map/while/body/eval_jaxpr/ppermute | solution.py:20
  247.9 16.4 %collective-permute-start = (bf16[16,16,512]{2,1,0:T(8,128)(2,1)}, bf16[16,16,512]{2,1,0:T(8,128)(2,1)S(1)}, u32[]{:S(2)}, u32[]{:S(2)}) collective-permute-start(bf16[16,16,512]{2,1,0:T(8,128)(2,1)} %get-tuple-element.507), channel_id=1, source_target_pairs={{0,128},{128,256},{256,384},{1,129},{129,257},{257,385},{2,130},{1... | collective-permute-start | bytes 786440 | tf_op jit(solution)/shard_map/while/body/eval_jaxpr/ppermute | solution.py:20
  265.2 172.1 %all-gather.10.cloned.1.call-start = ((), (), s32[]{:S(2)}) async-start(), calls=%async_computation.2 | async-start | bytes 6144000 | tf_op jit(solution)/shard_map/all_gather | solution.py:157
  318.0 6.0 %copy-start.4 = (bf16[196,256]{1,0:T(8,128)(2,1)S(1)}, bf16[196,256]{1,0:T(8,128)(2,1)}, u32[]{:S(2)}) copy-start(bf16[196,256]{1,0:T(8,128)(2,1)} %param.28) | copy-start | bytes 301060
  318.0 6.7 %copy-start.7 = (f32[2,1024]{1,0:T(2,128)S(1)}, f32[2,1024]{1,0:T(2,128)}, u32[]{:S(2)}) copy-start(f32[2,1024]{1,0:T(2,128)} %param.31) | copy-start | bytes 24580
  374.2 3.1 copy-start.2
  451.4 1.0 copy-start.3
  451.4 28.0 %copy-start.8 = (s32[1,4]{1,0:T(1,128)S(1)}, s32[1,4]{1,0:T(1,128)}, u32[]{:S(2)}) copy-start(s32[1,4]{1,0:T(1,128)} %param.33) | copy-start | bytes 52
  470.5 10.9 %collective-permute-start.1 = (f32[1,1024]{1,0:T(1,128)S(1)}, f32[1,1024]{1,0:T(1,128)S(1)}, u32[]{:S(2)}, u32[]{:S(2)}) collective-permute-start(f32[1,1024]{1,0:T(1,128)S(1)} %get-tuple-element.394), channel_id=1, source_target_pairs={{0,1},{1,2},{2,3},{3,4},{4,5},{5,6},{6,7},{7,8},{8,9},{9,10},{10,1... | collective-permute-start | bytes 12296 | tf_op jit(solution)/shard_map/ppermute | solution.py:33
  472.4 9.0 %collective-permute-start.2 = (f32[1,1024]{1,0:T(1,128)S(1)}, f32[1,1024]{1,0:T(1,128)S(1)}, u32[]{:S(2)}, u32[]{:S(2)}) collective-permute-start(f32[1,1024]{1,0:T(1,128)S(1)} %get-tuple-element.393), channel_id=1, source_target_pairs={{1,0},{2,1},{3,2},{4,3},{5,4},{6,5},{7,6},{8,7},{9,8},{10,9},{11,1... | collective-permute-start | bytes 12296 | tf_op jit(solution)/shard_map/ppermute | solution.py:36
Sparse Core Ops, SparseCore 0:
  10.5 86.0 all-gather.5
  99.7 79.7 all-gather.7
  265.3 44.5 all-gather.11
  377.4 59.8 all-gather.9
